TPU v7x, 32 devices: a whole 2x2x4 slice. The times are simulated.
32 devices in a mesh: dp: 8 (over z, x), mp: 4 (over y, core).
Axes of the slice: x: 2, y: 2, z: 4, core: 2. Of those that a mesh axis runs over, the one named last changes fastest.
Arguments:
- tokens: bfloat16 [8192, 1024], P(('dp', 'mp')), may hold values from -6 to 6
- w_query: bfloat16 [1024, 1024], P(None, 'mp'), may hold values from -0.046875 to 0.046875
- w_key: bfloat16 [1024, 1024], P(None, 'mp'), may hold values from -0.1875 to 0.1875
- w_value: bfloat16 [1024, 1024], P(None, 'mp'), may hold values from -0.1875 to 0.1875
- w_attn_out: bfloat16 [1024, 1024], P('mp'), may hold values from -1 to 1
- w_gate: bfloat16 [1024, 2816], P(None, 'mp'), may hold values from -0.1875 to 0.1875
- w_up: bfloat16 [1024, 2816], P(None, 'mp'), may hold values from -0.1875 to 0.1875
- w_down: bfloat16 [2816, 1024], P('mp'), may hold values from -0.109375 to 0.109375
- norm_attn: float32 [1024], replicated, may hold values from 0.1 to 1.9
- norm_ffn: float32 [1024], replicated, may hold values from 0.1 to 1.9
- rel_table: float32 [32, 16], P(None, 'mp'), may hold values from -3 to 3
- x_table: float32 [32, 16], P(None, 'mp'), may hold values from -3 to 3
- y_table: float32 [32, 16], P(None, 'mp'), may hold values from -3 to 3
- lengths: int32 [8, 2], P('dp'), may hold values from 0 to 1024, as said below
- boxes: int32 [2, 8192], P(None, 'dp'), may hold values from 0 to 127
- cotangent: bfloat16 [8192, 1024], P(('dp', 'mp')), may hold values from -6 to 6
Outputs:
- result: float32 [8192, 1024], P(('dp', 'mp'))
- d_tokens: float32 [8192, 1024], P(('dp', 'mp'))
- grad_query: float32 [1024, 1024], P('dp', 'mp')
- grad_key: float32 [1024, 1024], P('dp', 'mp')
- grad_value: float32 [1024, 1024], P('dp', 'mp')
- grad_attn_out: float32 [1024, 1024], P('mp', 'dp')
- grad_gate: float32 [1024, 2816], P('dp', 'mp')
- grad_up: float32 [1024, 2816], P('dp', 'mp')
- grad_down: float32 [2816, 1024], P('mp', 'dp')
- grad_norm_attn: float32 [1024], P(('dp', 'mp'))
- grad_norm_ffn: float32 [1024], P(('dp', 'mp'))
- grad_rel: float32 [32, 16], P('dp', 'mp')
- grad_x: float32 [32, 16], P('dp', 'mp')
- grad_y: float32 [32, 16], P('dp', 'mp')
Inputs may be any that keep to these rules, and one draw needn't show every extreme that they name: `lengths`: in a group whose index modulo 8 is under 5 the odd slots are 0 and the even slots hold 512 to 1024; in the other groups every slot holds 256 to 512. Group 0 has a sequence of 1024 and group 5 one of 512.
All inputs are finite; a program needn't handle non-finite values.
Results may differ from a plain program's by a relative error of at most 0.03.
Values may be sent and summed in bfloat16 or wider, within the bound.
No kernel may reach another device: no remote copies, remote signals or barrier semaphores. Data moves between devices by JAX's collectives and lax.ppermute only.
A program may use at most 832 MiB of HBM per device.

v0:
```python
import jax
import jax.numpy as jnp
from jax import lax
from jax.sharding import PartitionSpec as P

HEAD = 64
NB = 32
COORD = 128
LONG = 1024
SHORT = 512


thresholds = (1, 2, 3, 4, 5, 6, 7, 8, 12, 16, 23, 32, 46, 64, 91)
norm_eps = 1e-06
masked_score = -1000000000.0
highest = lax.Precision.HIGHEST


def bucket_of(offsets):
    distance = jnp.abs(offsets)
    bucket_ids = (offsets > 0).astype(jnp.int32) * (NB // 2)
    for threshold in thresholds:
        bucket_ids = bucket_ids + (distance >= threshold).astype(jnp.int32)
    return bucket_ids


def rms_norm(values, gain):
    return values * lax.rsqrt(jnp.mean(values * values, axis=-1, keepdims=True) + norm_eps) * gain


def contract(left_arr, right_arr, left_dim, right_dim):
    return lax.dot_general(
        left_arr,
        right_arr,
        (((left_dim,), (right_dim,)), ((), ())),
        preferred_element_type=jnp.float32,
    )


def frame_layout(slot_lengths, group_len):
    positions = jnp.arange(group_len, dtype=jnp.int32)
    slot_ids = jnp.arange(slot_lengths.shape[0], dtype=jnp.int32)
    slot_of = positions // SHORT
    own_length = jnp.sum(
        jnp.where(slot_of[:, None] == slot_ids[None, :], slot_lengths[None, :], 0), axis=1
    )
    seq_start = jnp.where(own_length > 0, slot_of, slot_of - 1)
    start_length = jnp.sum(
        jnp.where(seq_start[:, None] == slot_ids[None, :], slot_lengths[None, :], 0), axis=1
    )
    is_valid = positions - seq_start * SHORT < start_length
    return (seq_start, is_valid)


def frame_mask(seq_start, is_valid):
    positions = jnp.arange(seq_start.shape[0], dtype=jnp.int32)
    same_seq = (seq_start[:, None] == seq_start[None, :]) & is_valid[None, :]
    return same_seq | (positions[:, None] == positions[None, :])


def grid_one_hot():
    levels = jnp.arange(COORD, dtype=jnp.int32)
    bucket_ids = jnp.arange(NB, dtype=jnp.int32)
    grid_ids = bucket_of(levels[None, :] - levels[:, None])
    return (grid_ids[:, :, None] == bucket_ids[None, None, :]).astype(jnp.float32)


def level_hot(coords):
    levels = jnp.arange(COORD, dtype=jnp.int32)
    return (coords[:, None] == levels[None, :]).astype(jnp.bfloat16)


def layout_bias(table, coords, grid_hot):
    lookup = jnp.einsum("abn,nh->hab", grid_hot, table, precision=highest)
    query_rows = jnp.take(lookup, coords, axis=1)
    high_part = query_rows.astype(jnp.bfloat16)
    rest_part = (query_rows - high_part.astype(jnp.float32)).astype(jnp.bfloat16)
    key_hot = level_hot(coords)
    high_bias = jnp.einsum("hqb,kb->hqk", high_part, key_hot, preferred_element_type=jnp.float32)
    return high_bias + jnp.einsum(
        "hqb,kb->hqk", rest_part, key_hot, preferred_element_type=jnp.float32
    )


def layout_grad(d_scores, coords, grid_hot):
    key_hot = level_hot(coords)
    d_rows = jnp.einsum("hqk,kb->qhb", d_scores, key_hot, preferred_element_type=jnp.float32)
    d_lookup = jnp.einsum("qa,qhb->ahb", key_hot.astype(jnp.float32), d_rows, precision=highest)
    return jnp.einsum("ahb,abn->nh", d_lookup, grid_hot, precision=highest)


def offset_buckets(frame_len):
    positions = jnp.arange(frame_len, dtype=jnp.int32)
    return bucket_of(positions[None, :] - positions[:, None])


def relative_bias(rel_table, bucket_grid):
    return jnp.transpose(jnp.take(rel_table, bucket_grid, axis=0), (2, 0, 1))


def relative_grad(d_summed):
    local_heads, frame_len, _ = d_summed.shape
    widened = jnp.pad(d_summed, ((0, 0), (0, 0), (frame_len, 0)))
    flat_rows = widened.reshape(local_heads, 2 * frame_len * frame_len)
    flat_rows = jnp.pad(flat_rows, ((0, 0), (0, frame_len)))
    skewed = flat_rows.reshape(local_heads, frame_len, 2 * frame_len + 1)
    diagonal = jnp.sum(skewed, axis=1)
    offsets = jnp.arange(2 * frame_len + 1, dtype=jnp.int32) - frame_len
    bucket_ids = jnp.arange(NB, dtype=jnp.int32)
    offset_hot = (bucket_of(offsets)[:, None] == bucket_ids[None, :]).astype(jnp.float32)
    return jnp.einsum("tn,ht->nh", offset_hot, diagonal, precision=highest)


def frame_scores(queries, keys_in, bias_all, allowed):
    frame_len, width = queries.shape
    q_heads = queries.reshape(frame_len, width // HEAD, HEAD)
    k_heads = keys_in.reshape(frame_len, width // HEAD, HEAD)
    scores = (
        jnp.einsum("qhd,khd->hqk", q_heads, k_heads, preferred_element_type=jnp.float32) + bias_all
    )
    return (jnp.where(allowed[None], scores, masked_score), q_heads, k_heads)


def attend(queries, keys_in, values_in, bias_all, allowed):
    frame_len, width = queries.shape
    scores, q_heads, k_heads = frame_scores(queries, keys_in, bias_all, allowed)
    row_max = jnp.max(scores, axis=-1, keepdims=True)
    exponent = jnp.exp(scores - row_max)
    row_total = jnp.sum(exponent, axis=-1, keepdims=True)
    weights = (exponent / row_total).astype(jnp.bfloat16)
    v_heads = values_in.reshape(frame_len, width // HEAD, HEAD)
    context = jnp.einsum("hqk,khd->qhd", weights, v_heads, preferred_element_type=jnp.float32)
    return (context.reshape(frame_len, width).astype(jnp.bfloat16), row_max + jnp.log(row_total))


def attend_back(queries, keys_in, values_in, bias_all, allowed, log_total, d_context):
    frame_len, width = queries.shape
    scores, q_heads, k_heads = frame_scores(queries, keys_in, bias_all, allowed)
    weights = jnp.exp(scores - log_total)
    v_heads = values_in.reshape(frame_len, width // HEAD, HEAD)
    d_heads = d_context.reshape(frame_len, width // HEAD, HEAD)
    d_values = jnp.einsum(
        "hqk,qhd->khd", weights.astype(jnp.bfloat16), d_heads, preferred_element_type=jnp.float32
    )
    d_weights = jnp.einsum("qhd,khd->hqk", d_heads, v_heads, preferred_element_type=jnp.float32)
    d_scores = weights * (d_weights - jnp.sum(weights * d_weights, axis=-1, keepdims=True))
    d_scores = d_scores.astype(jnp.bfloat16)
    d_queries = jnp.einsum("hqk,khd->qhd", d_scores, k_heads, preferred_element_type=jnp.float32)
    d_keys = jnp.einsum("hqk,qhd->khd", d_scores, q_heads, preferred_element_type=jnp.float32)
    return (
        d_queries.reshape(frame_len, width).astype(jnp.bfloat16),
        d_keys.reshape(frame_len, width).astype(jnp.bfloat16),
        d_values.reshape(frame_len, width).astype(jnp.bfloat16),
        d_scores,
    )


def gated_unit(gate_proj, up_proj):
    return jax.nn.gelu(gate_proj, approximate=True) * up_proj


def local(
    tokens,
    w_query,
    w_key,
    w_value,
    w_attn_out,
    w_gate,
    w_up,
    w_down,
    norm_attn,
    norm_ffn,
    rel_table,
    x_table,
    y_table,
    lengths,
    boxes,
    cotangent,
):
    local_rows = tokens.shape[0]
    group_len = local_rows * lax.axis_size("mp")
    frames = group_len // LONG
    seq_start, is_valid = frame_layout(lengths[0], group_len)
    grid_hot = grid_one_hot()
    bucket_grid = offset_buckets(LONG)
    rel_part = relative_bias(rel_table, bucket_grid)

    def by_frame(array):
        return array.reshape((frames, LONG) + array.shape[1:])

    def frame_bias(coord_x, coord_y):
        return (
            rel_part
            + layout_bias(x_table, coord_x, grid_hot)
            + layout_bias(y_table, coord_y, grid_hot)
        )

    inputs = tokens.astype(jnp.float32)
    normed = lax.all_gather(
        rms_norm(inputs, norm_attn).astype(jnp.bfloat16), "mp", axis=0, tiled=True
    )
    queries = jnp.dot(normed, w_query, preferred_element_type=jnp.float32).astype(jnp.bfloat16)
    keys_all = jnp.dot(normed, w_key, preferred_element_type=jnp.float32).astype(jnp.bfloat16)
    values_all = jnp.dot(normed, w_value, preferred_element_type=jnp.float32).astype(jnp.bfloat16)
    frame_inputs = (
        by_frame(queries),
        by_frame(keys_all),
        by_frame(values_all),
        by_frame(seq_start),
        by_frame(is_valid),
        by_frame(boxes[0]),
        by_frame(boxes[1]),
    )

    def forward_frame(frame_args):
        q_part, k_part, v_part, start_part, valid_part, coord_x, coord_y = frame_args
        bias_all = frame_bias(coord_x, coord_y)
        return attend(q_part, k_part, v_part, bias_all, frame_mask(start_part, valid_part))

    context, log_total = lax.map(forward_frame, frame_inputs)
    context = context.reshape(group_len, context.shape[-1])
    rows_in = context
    mixed = inputs + lax.psum_scatter(
        jnp.dot(rows_in, w_attn_out, preferred_element_type=jnp.float32).astype(jnp.bfloat16),
        "mp",
        scatter_dimension=0,
        tiled=True,
    ).astype(jnp.float32)
    normed_ffn = lax.all_gather(
        rms_norm(mixed, norm_ffn).astype(jnp.bfloat16), "mp", axis=0, tiled=True
    )
    gate_proj = jnp.dot(normed_ffn, w_gate, preferred_element_type=jnp.float32)
    up_proj = jnp.dot(normed_ffn, w_up, preferred_element_type=jnp.float32)
    hidden = gated_unit(gate_proj, up_proj).astype(jnp.bfloat16)
    rows_in = hidden
    result = mixed + lax.psum_scatter(
        jnp.dot(rows_in, w_down, preferred_element_type=jnp.float32).astype(jnp.bfloat16),
        "mp",
        scatter_dimension=0,
        tiled=True,
    ).astype(jnp.float32)
    d_out = cotangent.astype(jnp.float32)
    d_full = lax.all_gather(cotangent, "mp", axis=0, tiled=True)
    d_hidden = contract(d_full, w_down, 1, 1)
    grad_down = contract(hidden, d_full, 0, 0)
    gelu_out, gelu_pull = jax.vjp(gated_unit, gate_proj, up_proj)
    d_gate, d_up = gelu_pull(d_hidden)
    d_gate = d_gate.astype(jnp.bfloat16)
    d_up = d_up.astype(jnp.bfloat16)
    grad_gate = contract(normed_ffn, d_gate, 0, 0)
    grad_up = contract(normed_ffn, d_up, 0, 0)
    d_normed_ffn = lax.psum_scatter(
        (contract(d_gate, w_gate, 1, 1) + contract(d_up, w_up, 1, 1)).astype(jnp.bfloat16),
        "mp",
        scatter_dimension=0,
        tiled=True,
    ).astype(jnp.float32)
    norm_out, norm_pull = jax.vjp(rms_norm, mixed, norm_ffn)
    d_mixed_part, grad_norm_ffn = norm_pull(d_normed_ffn)
    d_mixed = d_out + d_mixed_part
    d_attn = lax.all_gather(d_mixed.astype(jnp.bfloat16), "mp", axis=0, tiled=True)
    d_context = contract(d_attn, w_attn_out, 1, 1).astype(jnp.bfloat16)
    grad_attn_out = contract(context, d_attn, 0, 0)

    def backward_frame(running, frame_args):
        q_part, k_part, v_part, start_part, valid_part, coord_x, coord_y, log_part, d_part = (
            frame_args
        )
        bias_all = frame_bias(coord_x, coord_y)
        d_q, d_k, d_v, d_scores = attend_back(
            q_part, k_part, v_part, bias_all, frame_mask(start_part, valid_part), log_part, d_part
        )
        x_term = layout_grad(d_scores, coord_x, grid_hot)
        y_term = layout_grad(d_scores, coord_y, grid_hot)
        return (
            (running[0] + d_scores.astype(jnp.float32), running[1] + x_term, running[2] + y_term),
            (d_q, d_k, d_v),
        )

    zero_grads = (jnp.zeros_like(rel_part), jnp.zeros_like(x_table), jnp.zeros_like(y_table))
    table_grads, (d_queries, d_keys, d_values) = lax.scan(
        backward_frame, zero_grads, frame_inputs + (log_total, by_frame(d_context))
    )
    rel_grad = relative_grad(table_grads[0])
    d_queries = d_queries.reshape(group_len, d_queries.shape[-1])
    d_keys = d_keys.reshape(group_len, d_keys.shape[-1])
    d_values = d_values.reshape(group_len, d_values.shape[-1])
    grad_query = contract(normed, d_queries, 0, 0)
    grad_key = contract(normed, d_keys, 0, 0)
    grad_value = contract(normed, d_values, 0, 0)
    total_rows = contract(d_queries, w_query, 1, 1)
    total_rows = total_rows + contract(d_keys, w_key, 1, 1)
    d_normed = lax.psum_scatter(
        (total_rows + contract(d_values, w_value, 1, 1)).astype(jnp.bfloat16),
        "mp",
        scatter_dimension=0,
        tiled=True,
    ).astype(jnp.float32)
    first_out, first_pull = jax.vjp(rms_norm, inputs, norm_attn)
    d_inputs_part, grad_norm_attn = first_pull(d_normed)
    d_tokens = d_mixed + d_inputs_part
    gain_sums = (
        lax.psum_scatter(grad_norm_attn, ("dp", "mp"), scatter_dimension=0, tiled=True),
        lax.psum_scatter(grad_norm_ffn, ("dp", "mp"), scatter_dimension=0, tiled=True),
    )
    weight_sums = (
        lax.psum_scatter(
            grad_query.astype(jnp.bfloat16), "dp", scatter_dimension=0, tiled=True
        ).astype(jnp.float32),
        lax.psum_scatter(
            grad_key.astype(jnp.bfloat16), "dp", scatter_dimension=0, tiled=True
        ).astype(jnp.float32),
        lax.psum_scatter(
            grad_value.astype(jnp.bfloat16), "dp", scatter_dimension=0, tiled=True
        ).astype(jnp.float32),
        lax.psum_scatter(
            grad_attn_out.astype(jnp.bfloat16), "dp", scatter_dimension=1, tiled=True
        ).astype(jnp.float32),
        lax.psum_scatter(
            grad_gate.astype(jnp.bfloat16), "dp", scatter_dimension=0, tiled=True
        ).astype(jnp.float32),
        lax.psum_scatter(
            grad_up.astype(jnp.bfloat16), "dp", scatter_dimension=0, tiled=True
        ).astype(jnp.float32),
        lax.psum_scatter(
            grad_down.astype(jnp.bfloat16), "dp", scatter_dimension=1, tiled=True
        ).astype(jnp.float32),
        lax.psum_scatter(
            rel_grad.astype(jnp.bfloat16), "dp", scatter_dimension=0, tiled=True
        ).astype(jnp.float32),
        lax.psum_scatter(
            table_grads[1].astype(jnp.bfloat16), "dp", scatter_dimension=0, tiled=True
        ).astype(jnp.float32),
        lax.psum_scatter(
            table_grads[2].astype(jnp.bfloat16), "dp", scatter_dimension=0, tiled=True
        ).astype(jnp.float32),
    )
    return (
        result,
        d_tokens,
        weight_sums[0],
        weight_sums[1],
        weight_sums[2],
        weight_sums[3],
        weight_sums[4],
        weight_sums[5],
        weight_sums[6],
        gain_sums[0],
        gain_sums[1],
        weight_sums[7],
        weight_sums[8],
        weight_sums[9],
    )


def solution(mesh):
    in_specs = (
        P(("dp", "mp"), None),
        P(None, "mp"),
        P(None, "mp"),
        P(None, "mp"),
        P("mp", None),
        P(None, "mp"),
        P(None, "mp"),
        P("mp", None),
        P(),
        P(),
        P(None, "mp"),
        P(None, "mp"),
        P(None, "mp"),
        P("dp", None),
        P(None, "dp"),
        P(("dp", "mp"), None),
    )
    out_specs = (
        P(("dp", "mp"), None),
        P(("dp", "mp"), None),
        P("dp", "mp"),
        P("dp", "mp"),
        P("dp", "mp"),
        P("mp", "dp"),
        P("dp", "mp"),
        P("dp", "mp"),
        P("mp", "dp"),
        P(("dp", "mp")),
        P(("dp", "mp")),
        P("dp", "mp"),
        P("dp", "mp"),
        P("dp", "mp"),
    )
    return jax.shard_map(local, mesh=mesh, in_specs=in_specs, out_specs=out_specs, check_vma=False)
```

profile of v0, /device:TPU:0, one launch (start us, length us, event | category | flops | bytes accessed | tf_op | source)
XLA Modules:
  0.0 4926.3 jit_solution(14999315267508532215)
XLA Ops:
  9.7 2.0 fusion.77
  13.4 2.1 fusion.71
  15.5 4.5 gather_fusion.2
  20.0 4.5 bitcast_convert_fusion
  24.5 4.5 fusion.56
  30.5 4.5 gather_fusion.1
  35.0 4.5 bitcast_convert_fusion.1
  39.5 4.5 fusion.57
  43.9 8.5 fusion.9
  53.1 3.2 copy.122
  56.3 2.5 broadcast_clamp_fusion
  58.8 3771.3 %gather_fusion = f32[1048576,4]{1,0:T(8,128)} fusion(f32[32,4]{1,0:T(8,128)S(1)} %copy.73, s32[1048576]{0:T(1024)} %broadcast_clamp_fusion), kind=kCustom, calls=%fused_computation.2 | custom fusion | bytes 37748736 | tf_op jit(solution)/shard_map/jit(_take)/gather | solution.py:98
  3830.2 282.2 %copy.75 = f32[1024,1024,4]{0,1,2:T(8,128)} copy(f32[1024,1024,4]{2,1,0:T(8,128)} %bitcast.4) | data formatting | bytes 33554432 | tf_op jit(solution)/shard_map/jit(_take)/gather | solution.py:98
  4114.3 8.1 fusion.86
  4122.5 8.1 fusion.90
  4130.6 8.1 fusion.88
  4138.7 8.2 compare_and_fusion
  4146.9 2.4 convolution_convert_fusion.12
  4149.4 2.6 convolution_convert_fusion.13
  4152.8 8.1 fusion.168
  4160.9 34.8 fusion.167
  4195.8 8.1 fusion.3
  4204.7 7.5 fusion.65
  4212.3 2.1 convolution_convert_fusion
  4214.4 34.2 reduce-scatter.20.cloned.1.call-done
  4250.0 2.0 multiply_convert_fusion.3
  4252.7 22.1 all-gather.7.cloned.1.call-done
  4274.8 5.4 fusion.169
  4280.2 3.3 fusion.170
  4283.5 15.4 all-gather.9.cloned.1.call-done
  4298.9 7.4 multiply_convert_fusion.1
  4308.8 3.2 add_convert_fusion.1
  4312.1 31.5 reduce-scatter.24.cloned.1.call-done
  4343.6 2.1 fusion.79
  4346.3 2.2 fusion.165
  4348.6 3.7 convolution_convert_fusion.3
  4354.0 3.9 convolution_convert_fusion.2
  4359.6 3.7 convolution_convert_fusion.4
  4365.9 5.4 all-gather.11.cloned.1.call-done
  4371.3 2.5 convolution_convert_fusion.7
  4374.8 2.3 convolution_convert_fusion.11
  4377.2 10.8 multiply_reduce_fusion
  4388.0 12.1 multiply_convert_fusion
  4401.7 2.0 copy-done.1
  4405.4 6.2 convolution_convert_fusion.5
  4413.3 8.6 fusion.62
  4425.9 2.1 add_convert_fusion
  4429.4 3.3 convolution_convert_fusion.1
  4432.7 6.9 reduce-scatter.36.cloned.1.call-done
  4441.4 65.8 %reduce-scatter.38.cloned.1.call-done = bf16[128,704]{1,0:T(8,128)(2,1)} async-done(((bf16[1024,704]{1,0:T(8,128)(2,1)}), bf16[128,704]{1,0:T(8,128)(2,1)}) %reduce-scatter.38.cloned.1.call-update) | async-done | bytes 180240
  4509.0 65.3 %reduce-scatter.40.cloned.1.call-done = bf16[128,704]{1,0:T(8,128)(2,1)} async-done(((bf16[1024,704]{1,0:T(8,128)(2,1)}), bf16[128,704]{1,0:T(8,128)(2,1)}) %reduce-scatter.40.cloned.1.call-update) | async-done | bytes 180240
  4576.2 11.4 copy.121
  4587.6 6.5 pad_bitcast_fusion
  4594.1 40.1 copy.123
  4634.2 16.2 pad_convert_fusion
  4650.5 95.0 %reshape.617 = f32[8392704]{0:T(1024)} reshape(f32[4,2098176]{1,0:T(4,128)} %pad_convert_fusion) | data formatting | bytes 67141632
  4745.5 51.9 %reshape.563 = f32[4,1024,2049]{2,1,0:T(8,128)} reshape(f32[8392704]{0:T(1024)} %reshape.617) | data formatting | bytes 67141632 | tf_op jit(solution)/shard_map/reshape | solution.py:106
  4797.3 12.4 reduce_sum.120
  4811.4 4.7 fusion.100
  4819.2 4.7 fusion.106
  4827.1 36.1 all-reduce.8
  4873.4 2.1 fusion.80
  4875.5 37.3 all-reduce.7
  4916.1 3.3 fusion.82
  (209 shorter events, 57.9 us)
Async XLA Ops:
  7.2 4291.8 %copy-start = (bf16[704,1024]{1,0:T(8,128)(2,1)S(1)}, bf16[704,1024]{1,0:T(8,128)(2,1)}, u32[]{:S(2)}) copy-start(bf16[704,1024]{1,0:T(8,128)(2,1)} %param.25) | copy-start | bytes 4325380
  7.2 4139.7 %all-gather.5.cloned.1.call-start = ((), (), s32[]{:S(2)}) async-start(), calls=%async_computation.11 | async-start | bytes 2621440 | tf_op jit(solution)/shard_map/all_gather | solution.py:199
  11.8 4236.9 %reduce-scatter.20.cloned.1.call-start = ((), (), s32[]{:S(2)}) async-start(), calls=%async_computation.12 | async-start | bytes 2621440 | tf_op jit(solution)/shard_map/reduce_scatter | solution.py:223
  12.8 16.2 copy-start.26
  20.0 9.0 copy-start.31
  20.0 9.0 copy-start.54
  39.4 13.6 copy-start.44
  3830.1 282.2 %copy-start.40 = (s32[1024]{0:T(1024)S(1)}, s32[1024]{0:T(1024)}, u32[]{:S(2)}) copy-start(s32[1024]{0:T(1024)} %add_select_fusion.1) | copy-start | bytes 12292
  3830.2 282.2 %copy-start.45 = (s32[1,2]{1,0:T(1,128)S(1)}, s32[1,2]{1,0:T(1,128)}, u32[]{:S(2)}) copy-start(s32[1,2]{1,0:T(1,128)} %param.31) | copy-start | bytes 28
  3830.2 284.1 %copy-start.6 = (bf16[4,1024,128]{2,0,1:T(4,128)(2,1)S(1)}, bf16[4,1024,128]{2,0,1:T(4,128)(2,1)}, u32[]{:S(2)}) copy-start(bf16[4,1024,128]{2,0,1:T(4,128)(2,1)} %bitcast_convert_fusion) | copy-start | bytes 3145732
  3830.2 284.1 %copy-start.24 = (s32[1,1024]{1,0:T(1,128)S(1)}, s32[1,1024]{1,0:T(1,128)}, u32[]{:S(2)}) copy-start(s32[1,1024]{1,0:T(1,128)} %copy-done.23) | copy-start | bytes 12292
  4114.3 8.2 copy-start.8
  4114.3 8.1 copy-start.27
  4122.5 8.1 copy-start.7
  4149.4 2.6 copy-start.14
  4195.8 8.1 copy-start.18
  4195.8 8.2 copy-start.46
  4195.8 8.9 copy-start.29
  4203.9 8.3 copy-start.35
  4204.7 7.5 copy-start.20
  4212.2 39.9 copy-start.22
  4212.2 36.5 copy-start.2
  4212.2 37.8 copy-start.33
  4214.4 60.4 %all-gather.7.cloned.1.call-start = ((), (), s32[]{:S(2)}) async-start(), calls=%async_computation.13 | async-start | bytes 2621440 | tf_op jit(solution)/shard_map/all_gather | solution.py:229
  4250.0 95.7 %copy-start.37 = (f32[256]{0:T(256)}, f32[256]{0:T(256)S(1)}, u32[]{:S(2)}) copy-start(f32[256]{0:T(256)S(1)} %fusion.164) | copy-start | bytes 3076
  4252.1 46.9 all-gather.9.cloned.1.call-start
  4252.7 91.0 %reduce-scatter.24.cloned.1.call-start = ((), (), s32[]{:S(2)}) async-start(), calls=%async_computation.16 | async-start | bytes 2621440 | tf_op jit(solution)/shard_map/reduce_scatter | solution.py:252
  4274.8 5.4 copy-start.50
  4274.8 5.4 copy-start.52
  4298.9 7.4 copy-start.51
  4306.4 1.9 copy-start.57
  4306.4 2.4 copy-start.53
  4308.8 34.8 copy-start.4
  4308.8 37.5 copy-start.9
  4312.0 59.3 %all-gather.11.cloned.1.call-start = ((), (), s32[]{:S(2)}) async-start(), calls=%async_computation.17 | async-start | bytes 2621440 | tf_op jit(solution)/shard_map/all_gather | solution.py:261
  4348.6 91.0 %reduce-scatter.36.cloned.1.call-start = ((), (), s32[]{:S(2)}) async-start(), calls=%async_computation.23 | async-start | bytes 1769472
  4353.9 153.2 %reduce-scatter.38.cloned.1.call-start = ((), (), s32[]{:S(2)}) async-start(), calls=%async_computation.24 | async-start | bytes 1769472
  4359.5 214.8 %reduce-scatter.40.cloned.1.call-start = ((), (), s32[]{:S(2)}) async-start(), calls=%async_computation.25 | async-start | bytes 1769472
  4364.9 10.0 copy-start.21
  4364.9 500.9 %reduce-scatter.34.cloned.1.call-start = ((), (), s32[]{:S(2)}) async-start(), calls=%async_computation.22 | async-start | bytes 589824
  4387.9 480.9 %reduce-scatter.28.cloned.1.call-start = ((), (), s32[]{:S(2)}) async-start(), calls=%async_computation.19 | async-start | bytes 589824 | tf_op jit(solution)/shard_map/reduce_scatter | solution.py:307
  4388.0 12.1 copy-start.15
  4400.1 3.6 copy-start.1
  4400.2 3.6 copy-start.47
  4405.3 465.0 %reduce-scatter.30.cloned.1.call-start = ((), (), s32[]{:S(2)}) async-start(), calls=%async_computation.20 | async-start | bytes 589824 | tf_op jit(solution)/shard_map/reduce_scatter | solution.py:310
  4405.4 6.2 copy-start.48
  4413.2 458.6 %reduce-scatter.32.cloned.1.call-start = ((), (), s32[]{:S(2)}) async-start(), calls=%async_computation.21 | async-start | bytes 589824 | tf_op jit(solution)/shard_map/reduce_scatter | solution.py:313
  4413.3 8.7 copy-start.49
  4421.9 2.1 copy-start.16
  4423.6 449.8 %reduce-scatter.26.cloned.1.call-start = ((), (), s32[]{:S(2)}) async-start(), calls=%async_computation.18 | async-start | bytes 2621440 | tf_op jit(solution)/shard_map/reduce_scatter | solution.py:293
  4425.9 2.2 copy-start.55
  4425.9 3.5 copy-start.58
  4428.1 488.0 %reduce-scatter.22.cloned.1.call-start = ((), (), s32[]{:S(2)}) async-start(), calls=%async_computation.14 | async-start | bytes 2621440 | tf_op jit(solution)/shard_map/reduce_scatter | solution.py:236
  4797.3 14.1 copy-start.28
  4811.4 6.0 copy-start.32
  4811.4 7.8 copy-start.25
  4823.9 49.4 %copy-start.3 = (bf16[256,1024]{1,0:T(8,128)(2,1)S(1)}, bf16[256,1024]{1,0:T(8,128)(2,1)}, u32[]{:S(2)}) copy-start(bf16[256,1024]{1,0:T(8,128)(2,1)} %param.18) | copy-start | bytes 1572868
  4823.9 49.4 %copy-start.36 = (f32[1024]{0:T(1024)S(1)}, f32[1024]{0:T(1024)}, u32[]{:S(2)}) copy-start(f32[1024]{0:T(1024)} %param.26) | copy-start | bytes 12292
  4823.9 51.6 %copy-start.39 = (f32[1024]{0:T(1024)S(1)}, f32[1024]{0:T(1024)}, u32[]{:S(2)}) copy-start(f32[1024]{0:T(1024)} %get-tuple-element.97) | copy-start | bytes 12292
  4823.9 92.1 %copy-start.5 = (bf16[256,1024]{1,0:T(8,128)(2,1)S(1)}, bf16[256,1024]{1,0:T(8,128)(2,1)}, u32[]{:S(2)}) copy-start(bf16[256,1024]{1,0:T(8,128)(2,1)} %reduce-scatter.20.cloned.1.call-done) | copy-start | bytes 1572868
  4823.9 92.1 %copy-start.10 = (bf16[256,1024]{1,0:T(8,128)(2,1)S(1)}, bf16[256,1024]{1,0:T(8,128)(2,1)}, u32[]{:S(2)}) copy-start(bf16[256,1024]{1,0:T(8,128)(2,1)} %param.33) | copy-start | bytes 1572868
  4824.0 92.1 %copy-start.11 = (bf16[256,1024]{1,0:T(8,128)(2,1)S(1)}, bf16[256,1024]{1,0:T(8,128)(2,1)}, u32[]{:S(2)}) copy-start(bf16[256,1024]{1,0:T(8,128)(2,1)} %reduce-scatter.24.cloned.1.call-done) | copy-start | bytes 1572868
  4824.0 92.1 %copy-start.34 = (f32[1024]{0:T(1024)S(1)}, f32[1024]{0:T(1024)}, u32[]{:S(2)}) copy-start(f32[1024]{0:T(1024)} %param.27) | copy-start | bytes 12292
  4824.0 92.1 %copy-start.38 = (f32[256]{0:T(256)S(1)}, f32[256]{0:T(256)}, u32[]{:S(2)}) copy-start(f32[256]{0:T(256)} %copy-done.37) | copy-start | bytes 3076
  (10 other events, 10.9 us)
Sparse Core Ops, SparseCore 0:
  11.9 25.2 all-gather.4
  4214.5 34.1 reduce-scatter.19
  4252.2 22.5 all-gather.6
  4276.3 22.5 all-gather.8
  4312.2 31.4 reduce-scatter.23
  4348.7 22.5 all-gather.10
  4374.7 64.7 reduce-scatter.35
  4443.4 63.7 reduce-scatter.37
  4510.6 63.6 reduce-scatter.39
  4577.9 60.8 reduce-scatter.33
  4642.7 60.8 reduce-scatter.27
  4707.8 60.8 reduce-scatter.29
  4772.0 60.9 reduce-scatter.31
  4835.5 30.4 reduce-scatter.25
  4868.4 31.4 reduce-scatter.21
where the time goes:
time: 5020 us; the launch traced here: 4930 us
  local copies, waits for them, and re-layouts  4290 us (85%)
  waiting for transfers between devices  247 us (5%)
  matrix products  180 us (4%)
  other arithmetic  117 us (2%)
  blocking collectives  73.4 us (1%)
    gather x2, local copies, waits for them, and re-layouts, relative_bias(): return jnp.transpose(jnp.take(rel_table, bucket_grid, axis=0), (2, 0, 1))  4050 us
    unnamed x135, local copies, waits for them, and re-layouts  176 us
    unnamed x19, waiting for transfers between devices  139 us
  transfers between devices with their start and end apart: 15, of which 8 were waited for; matrix products, arithmetic and copies ran while one was open for 91% of the time, Pallas kernels for 0%

commit v1 on v0

v1 whole, which is shorter than its diff:
```python
import functools

import jax
import jax.numpy as jnp
from jax import lax
from jax.experimental import pallas as pl
from jax.experimental.pallas import tpu as pltpu
from jax.sharding import PartitionSpec as P

f32, bf16, i32 = jnp.float32, jnp.bfloat16, jnp.int32
HEAD = 64
NB = 32
COORD = 128
SHORT = 512
NEAR = 3 * COORD
thresholds = (1, 2, 3, 4, 5, 6, 7, 8, 12, 16, 23, 32, 46, 64, 91)
masked_score = -1000000000.0


def dot(a, b):
    return jnp.dot(a, b, preferred_element_type=f32)


def bucket_of(offsets):
    distance = jnp.abs(offsets)
    bucket_ids = jnp.where(offsets > 0, NB // 2, 0)
    for threshold in thresholds:
        bucket_ids = bucket_ids + jnp.where(distance >= threshold, 1, 0)
    return bucket_ids


def offset_hot():
    offsets = lax.broadcasted_iota(i32, (NB, 512), 1) - 256
    return (bucket_of(offsets) == lax.broadcasted_iota(i32, (NB, 512), 0)).astype(f32)


def toeplitz(row, base):
    wide = jnp.broadcast_to(row, (COORD, 512))
    return pltpu.roll(wide, (256 - base) % 512, 1, stride=1, stride_axis=0)


def start_of(len0, len1):
    return jnp.where(len1 > 0, 1, 0), jnp.where(len1 > 0, len1, len0)


def build(lens, tab_ref, box_cols, box_rows, k_ref, b_scr, hot_scr, lut_scr, strip_scr, n_heads):
    n_keys = k_ref.shape[0]
    len0, len1 = lens[0, 0], lens[0, 1]
    start1, start1_len = start_of(len0, len1)
    lane = lax.broadcasted_iota(i32, (n_keys, COORD), 1)
    pos = lax.broadcasted_iota(i32, (n_keys, COORD), 0)
    x_hot = (box_cols[:, 0:1] == lane).astype(bf16)
    y_hot = (box_cols[:, 1:2] == lane).astype(bf16)
    second = pos >= SHORT
    start_k = jnp.where(second, start1, 0)
    limit = jnp.where(second, start1_len, len0)
    valid = pos - start_k * SHORT < limit
    masked0 = jnp.where(valid & (start_k == 0), 0.0, masked_score)
    masked1 = jnp.where(valid & (start_k == start1), 0.0, masked_score)
    extra = jnp.where(lane == 0, masked0, jnp.where(lane == 1, masked1, jnp.where(lane < 5, -1.0, 0.0)))
    extra = extra.astype(bf16)
    for pair in range(n_heads // 2):
        b_scr[pair, :, 0:128] = k_ref[:, pair * 128 : pair * 128 + 128]
        b_scr[pair, :, 128:256] = x_hot
        b_scr[pair, :, 256:384] = y_hot
        b_scr[pair, :, 384:512] = extra
    level = lax.broadcasted_iota(i32, (COORD, n_keys), 0)
    hot_scr[0:128, :] = (box_rows[0:1, :] == level).astype(bf16)
    hot_scr[128:256, :] = (box_rows[1:2, :] == level).astype(bf16)
    vec = jnp.dot(tab_ref[...], offset_hot(), precision=lax.Precision.HIGHEST, preferred_element_type=f32)
    n_strip = strip_scr.shape[1]
    for h in range(n_heads):
        for axis in range(2):
            at = n_heads * (1 + axis) + h
            table = toeplitz(vec[at : at + 1, :], 0)[:, 0:128]
            lut_scr[h, axis] = table.T.astype(bf16)
        near = toeplitz(vec[h : h + 1, :], -128)[:, 0:NEAR]
        mid = (n_strip - NEAR) // 2
        left = jnp.broadcast_to(vec[h : h + 1, 0:1], (mid, COORD))
        right = jnp.broadcast_to(vec[h : h + 1, 511:512], (mid, COORD))
        strip_scr[h, 0:mid, :] = left
        strip_scr[h, mid : mid + NEAR, :] = near.T
        strip_scr[h, mid + NEAR :, :] = right


def query_side(lens, block, qb, h, qt, hot_q, lut_scr, log_rows):
    half = jnp.zeros((HEAD, qb), bf16)
    own = qt[(h % 2) * HEAD : (h % 2) * HEAD + HEAD, :]
    parts = [own, half] if h % 2 == 0 else [half, own]
    x_rows = dot(lut_scr[h, 0], hot_q[0:128, :]).astype(bf16)
    y_rows = dot(lut_scr[h, 1], hot_q[128:256, :]).astype(bf16)
    row = lax.broadcasted_iota(i32, (128, qb), 0)
    q_pos = block * qb + lax.broadcasted_iota(i32, (128, qb), 1)
    slot = jnp.where(q_pos >= SHORT, 1, 0)
    extra = jnp.where(row == slot, 1.0, 0.0)
    if log_rows is not None:
        for piece, value in enumerate(log_rows):
            extra = jnp.where(row == 2 + piece, value, extra)
    return jnp.concatenate(parts + [x_rows, y_rows, extra.astype(bf16)], axis=0)


def pieces(value):
    high = value.astype(bf16).astype(f32)
    rest = value - high
    mid = rest.astype(bf16).astype(f32)
    return high, mid, (rest - mid).astype(bf16).astype(f32)


def scores(lens, block, qb, h, at, b_scr, strip_scr, s_scr):
    n_keys = b_scr.shape[1]
    s = dot(b_scr[h // 2], at)
    blocks = qb // COORD
    top = n_keys // COORD - 1
    for t in range(blocks):
        off = pl.multiple_of((top - (block * blocks + t)) * COORD, COORD)
        s_scr[:, t * 128 : t * 128 + 128] = s[:, t * 128 : t * 128 + 128] + strip_scr[h, pl.ds(off, n_keys), :]
    len0, len1 = lens[0, 0], lens[0, 1]
    start1, start1_len = start_of(len0, len1)
    last = block * qb + qb - 1
    in_second = last >= SHORT
    begin = jnp.where(in_second, start1, 0) * SHORT
    limit = jnp.where(in_second, start1_len, len0)

    @pl.when(last - begin >= limit)
    def _():
        row = lax.broadcasted_iota(i32, at.shape, 0)
        open_at = jnp.where((row == 384) | (row == 385), 0.0, at.astype(f32)).astype(bf16)
        eye = lax.broadcasted_iota(i32, (128, 128), 0) == lax.broadcasted_iota(i32, (128, 128), 1)
        for t in range(blocks):
            rows = pl.ds(pl.multiple_of((block * blocks + t) * 128, 128), 128)
            cols = slice(t * 128, t * 128 + 128)
            own = dot(b_scr[h // 2, rows, :], open_at[:, cols]) + strip_scr[h, top * 128 : top * 128 + 128, :]
            s_scr[rows, cols] = jnp.where(eye, own, s_scr[rows, cols])


def fwd_kernel(n_heads, qb, lens, tab_ref, box_cols, box_rows, q_ref, k_ref, v_ref, ctx_ref, ctxt_ref, lse_ref,
               b_scr, hot_scr, lut_scr, strip_scr, vt_scr, s_scr):
    block = pl.program_id(0)

    @pl.when(block == 0)
    def _():
        build(lens, tab_ref, box_cols, box_rows, k_ref, b_scr, hot_scr, lut_scr, strip_scr, n_heads)
        for pair in range(n_heads // 2):
            vt_scr[pair, 0:128, :] = v_ref[:, pair * 128 : pair * 128 + 128].T
            vt_scr[pair, 128:144, :] = jnp.ones((16, v_ref.shape[0]), bf16)

    hot_q = hot_scr[:, pl.ds(pl.multiple_of(block * qb, qb), qb)]
    for pair in range(n_heads // 2):
        qt = q_ref[:, pair * 128 : pair * 128 + 128].T
        halves = []
        for h in (2 * pair, 2 * pair + 1):
            at = query_side(lens, block, qb, h, qt, hot_q, lut_scr, None)
            scores(lens, block, qb, h, at, b_scr, strip_scr, s_scr)
            s = s_scr[...]
            top = jnp.max(s, axis=0, keepdims=True)
            p = jnp.exp(s - top).astype(bf16)
            out = dot(vt_scr[pair], p)
            total = out[128:129, :]
            halves.append(out[(h % 2) * HEAD : (h % 2) * HEAD + HEAD, :] / total)
            lse_ref[h : h + 1, :] = top + jnp.log(total)
        ctxt = jnp.concatenate(halves, axis=0)
        ctxt_ref[pair * 128 : pair * 128 + 128, :] = ctxt
        ctx_ref[:, pair * 128 : pair * 128 + 128] = ctxt.T.astype(bf16)


def scratch(n_keys, n_heads):
    return [
        pltpu.VMEM((n_heads // 2, n_keys, 512), bf16),
        pltpu.VMEM((256, n_keys), bf16),
        pltpu.VMEM((n_heads, 2, COORD, COORD), bf16),
        pltpu.VMEM((n_heads, 2 * n_keys - COORD, COORD), f32),
    ]


def whole(shape):
    return pl.BlockSpec(shape, lambda i: (0,) * len(shape))


def attend(q, k, v, tables, lengths, box_cols, box_rows, qb=256):
    n_keys, width = k.shape
    n_rows = q.shape[0]
    n_heads = width // HEAD
    return pl.pallas_call(
        functools.partial(fwd_kernel, n_heads, qb),
        out_shape=(
            jax.ShapeDtypeStruct((n_rows, width), bf16),
            jax.ShapeDtypeStruct((width, n_rows), f32),
            jax.ShapeDtypeStruct((8, n_rows), f32),
        ),
        grid=(n_rows // qb,),
        in_specs=[
            pl.BlockSpec(memory_space=pltpu.SMEM),
            whole(tables.shape), whole(box_cols.shape), whole(box_rows.shape),
            pl.BlockSpec((qb, width), lambda i: (i, 0)), whole(k.shape), whole(v.shape),
        ],
        out_specs=(
            pl.BlockSpec((qb, width), lambda i: (i, 0)),
            pl.BlockSpec((width, qb), lambda i: (0, i)),
            pl.BlockSpec((8, qb), lambda i: (0, i)),
        ),
        scratch_shapes=scratch(n_keys, n_heads) + [
            pltpu.VMEM((n_heads // 2, 144, n_keys), bf16),
            pltpu.VMEM((n_keys, qb), f32),
        ],
        compiler_params=pltpu.CompilerParams(dimension_semantics=("arbitrary",), vmem_limit_bytes=56 << 20),
        cost_estimate=pl.CostEstimate(flops=8 * n_heads * n_rows * n_keys * 512, bytes_accessed=4 << 20, transcendentals=n_heads * n_rows * n_keys),
        name="attend",
    )(lengths, tables, box_cols, box_rows, q, k, v)


def skew_sums(tile, base):
    width = tile.shape[1]
    wide = jnp.concatenate([tile, jnp.zeros((128, 512 - width), f32)], axis=1)
    row = lax.broadcasted_iota(i32, (128, 512), 0)
    for bit in range(7):
        wide = jnp.where((row >> bit) & 1 == 1, pltpu.roll(wide, 512 - (1 << bit), 1), wide)
    sums = jnp.sum(wide, axis=0, keepdims=True)
    return pltpu.roll(jnp.broadcast_to(sums, (8, 512)), (256 + base) % 512, 1)[0:1, :]


def bwd_kernel(n_heads, qb, lens, tab_ref, box_cols, box_rows, q_ref, k_ref, v_ref, do_ref, ctxt_ref, lse_ref,
               dq_ref, dk_ref, dv_ref, dtab_ref,
               b_scr, hot_scr, lut_scr, strip_scr, v_scr, kt_scr, s_scr, p_scr, ds_scr, dk_scr, dv_scr, near_scr, lut_acc, far_acc):
    block = pl.program_id(0)
    n_keys = k_ref.shape[0]
    blocks = qb // COORD
    key_blocks = n_keys // COORD

    @pl.when(block == 0)
    def _():
        build(lens, tab_ref, box_cols, box_rows, k_ref, b_scr, hot_scr, lut_scr, strip_scr, n_heads)
        lane = lax.broadcasted_iota(i32, (n_keys, 128), 1)
        minus = jnp.where(lane < 3, -1.0, 0.0).astype(bf16)
        kb = lax.broadcasted_iota(i32, (16, n_keys), 0)
        kp = lax.broadcasted_iota(i32, (16, n_keys), 1)
        for pair in range(n_heads // 2):
            v_scr[pair, :, 0:128] = v_ref[:, pair * 128 : pair * 128 + 128]
            v_scr[pair, :, 128:256] = minus
            kt_scr[pair, 0:128, :] = k_ref[:, pair * 128 : pair * 128 + 128].T
            kt_scr[pair, 128:384, :] = hot_scr[...]
            kt_scr[pair, 384:400, :] = (kp // COORD == kb).astype(bf16)
        dk_scr[...] = jnp.zeros_like(dk_scr)
        dv_scr[...] = jnp.zeros_like(dv_scr)
        near_scr[...] = jnp.zeros_like(near_scr)
        lut_acc[...] = jnp.zeros_like(lut_acc)
        far_acc[...] = jnp.zeros_like(far_acc)
        ds_scr[0:128, :] = jnp.zeros((128, 2 * qb), bf16)
        ds_scr[128 + n_keys :, :] = jnp.zeros((128, 2 * qb), bf16)

    hot_q = hot_scr[:, pl.ds(pl.multiple_of(block * qb, qb), qb)]
    rows_q = pl.ds(pl.multiple_of(block * qb, qb), qb)
    lane_half = lax.broadcasted_iota(i32, (qb, 128), 1) >= HEAD
    for pair in range(n_heads // 2):
        cols = slice(pair * 128, pair * 128 + 128)
        q = q_ref[:, cols]
        do = do_ref[:, cols]
        qt, dot_t = q.T, do.T
        prod = dot_t.astype(f32) * ctxt_ref[cols, :]
        dq_halves = []
        for sub in range(2):
            h = 2 * pair + sub
            mine = slice(sub * HEAD, sub * HEAD + HEAD)
            delta = jnp.sum(prod[mine, :], axis=0, keepdims=True)
            at = query_side(lens, block, qb, h, qt, hot_q, lut_scr, pieces(lse_ref[h : h + 1, :]))
            scores(lens, block, qb, h, at, b_scr, strip_scr, s_scr)
            p = jnp.exp(s_scr[...])
            row = lax.broadcasted_iota(i32, (128, qb), 0)
            extra = jnp.zeros((128, qb), f32)
            for piece, value in enumerate(pieces(delta)):
                extra = jnp.where(row == piece, value, extra)
            none = jnp.zeros((HEAD, qb), bf16)
            own = dot_t[mine, :]
            dat = jnp.concatenate([own, none] if sub == 0 else [none, own], axis=0)
            dp = dot(v_scr[pair], jnp.concatenate([dat, extra.astype(bf16)], axis=0))
            ds = (p * dp).astype(bf16)
            p_scr[:, sub * qb : sub * qb + qb] = p.astype(bf16)
            ds_scr[128 : 128 + n_keys, sub * qb : sub * qb + qb] = ds
            got = dot(kt_scr[pair], ds)
            dq_halves.append(got[mine, :])
            for axis in range(2):
                part = got[128 + 128 * axis : 256 + 128 * axis, :].astype(bf16)
                lut_acc[h, axis] += dot(part, b_scr[pair, rows_q, 128 + 128 * axis : 256 + 128 * axis])
            by_block = got[384:392, :]
            key_block = lax.broadcasted_iota(i32, (8, qb), 0)
            q_block = block * blocks + lax.broadcasted_iota(i32, (8, qb), 1) // COORD
            far_acc[h, 0] += jnp.where(key_block + 1 < q_block, by_block, 0.0)
            far_acc[h, 1] += jnp.where(key_block > q_block + 1, by_block, 0.0)
            for t in range(blocks):
                rows = pl.ds(pl.multiple_of((block * blocks + t) * COORD, COORD), NEAR)
                near_scr[h] += ds_scr[rows, sub * qb + t * 128 : sub * qb + t * 128 + 128].astype(f32)
        dq_ref[:, cols] = jnp.concatenate(dq_halves, axis=0).T.astype(bf16)

        def both(x):
            return jnp.concatenate([jnp.where(lane_half, 0.0, x.astype(f32)), jnp.where(lane_half, x.astype(f32), 0.0)], axis=0).astype(bf16)

        dv_scr[pair] += dot(p_scr[...], both(do))
        dk_scr[pair] += dot(ds_scr[128 : 128 + n_keys, :], both(q))

    @pl.when(block == pl.num_programs(0) - 1)
    def _():
        for pair in range(n_heads // 2):
            cols = slice(pair * 128, pair * 128 + 128)
            dk_ref[:, cols] = dk_scr[pair].astype(bf16)
            dv_ref[:, cols] = dv_scr[pair].astype(bf16)
        offset = lax.broadcasted_iota(i32, (1, 512), 1) - 256
        sums = []
        for h in range(n_heads):
            near = skew_sums(near_scr[h].T, -128)
            left = jnp.sum(far_acc[h, 0], keepdims=True)
            right = jnp.sum(far_acc[h, 1], keepdims=True)
            sums.append(near + jnp.where(offset == -256, left, 0.0) + jnp.where(offset == 255, right, 0.0))
        for axis in range(2):
            for h in range(n_heads):
                sums.append(skew_sums(lut_acc[h, axis].T, 0))
        sums = jnp.concatenate(sums + [jnp.zeros((16 - len(sums), 512), f32)], axis=0)
        dtab_ref[...] = lax.dot_general(offset_hot(), sums, (((1,), (1,)), ((), ())), precision=lax.Precision.HIGHEST, preferred_element_type=f32)


def attend_back(q, k, v, d_ctx, ctxt, lse, tables, lengths, box_cols, box_rows, qb=256):
    n_keys, width = k.shape
    n_rows = q.shape[0]
    n_heads = width // HEAD
    return pl.pallas_call(
        functools.partial(bwd_kernel, n_heads, qb),
        out_shape=(
            jax.ShapeDtypeStruct((n_rows, width), bf16),
            jax.ShapeDtypeStruct((n_keys, width), bf16),
            jax.ShapeDtypeStruct((n_keys, width), bf16),
            jax.ShapeDtypeStruct((NB, 16), f32),
        ),
        grid=(n_rows // qb,),
        in_specs=[
            pl.BlockSpec(memory_space=pltpu.SMEM),
            whole(tables.shape), whole(box_cols.shape), whole(box_rows.shape),
            pl.BlockSpec((qb, width), lambda i: (i, 0)), whole(k.shape), whole(v.shape),
            pl.BlockSpec((qb, width), lambda i: (i, 0)),
            pl.BlockSpec((width, qb), lambda i: (0, i)),
            pl.BlockSpec((8, qb), lambda i: (0, i)),
        ],
        out_specs=(
            pl.BlockSpec((qb, width), lambda i: (i, 0)),
            whole(k.shape), whole(v.shape), whole((NB, 16)),
        ),
        scratch_shapes=scratch(n_keys, n_heads) + [
            pltpu.VMEM((n_heads // 2, n_keys, 256), bf16),
            pltpu.VMEM((n_heads // 2, 400, n_keys), bf16),
            pltpu.VMEM((n_keys, qb), f32),
            pltpu.VMEM((n_keys, 2 * qb), bf16),
            pltpu.VMEM((n_keys + 256, 2 * qb), bf16),
            pltpu.VMEM((n_heads // 2, n_keys, 128), f32),
            pltpu.VMEM((n_heads // 2, n_keys, 128), f32),
            pltpu.VMEM((n_heads, NEAR, COORD), f32),
            pltpu.VMEM((n_heads, 2, COORD, COORD), f32),
            pltpu.VMEM((n_heads, 2, 8, qb), f32),
        ],
        compiler_params=pltpu.CompilerParams(dimension_semantics=("arbitrary",), vmem_limit_bytes=56 << 20),
        cost_estimate=pl.CostEstimate(flops=16 * n_heads * n_rows * n_keys * 512, bytes_accessed=8 << 20, transcendentals=n_heads * n_rows * n_keys),
        name="attend_back",
    )(lengths, tables, box_cols, box_rows, q, k, v, d_ctx, ctxt, lse)


norm_eps = 1e-06


def rms_norm(values, gain):
    return values * lax.rsqrt(jnp.mean(values * values, axis=-1, keepdims=True) + norm_eps) * gain


def contract(left_arr, right_arr, left_dim, right_dim):
    return lax.dot_general(
        left_arr, right_arr, (((left_dim,), (right_dim,)), ((), ())), preferred_element_type=f32
    )


def gated_unit(gate_proj, up_proj):
    return jax.nn.gelu(gate_proj, approximate=True) * up_proj


def local(
    tokens, w_query, w_key, w_value, w_attn_out, w_gate, w_up, w_down, norm_attn, norm_ffn,
    rel_table, x_table, y_table, lengths, boxes, cotangent,
):
    inputs = tokens.astype(f32)
    normed = lax.all_gather(rms_norm(inputs, norm_attn).astype(bf16), "mp", axis=0, tiled=True)
    queries = dot(normed, w_query).astype(bf16)
    keys_all = dot(normed, w_key).astype(bf16)
    values_all = dot(normed, w_value).astype(bf16)
    n_heads = w_query.shape[1] // HEAD
    tables = jnp.concatenate([rel_table.T, x_table.T, y_table.T, jnp.zeros((16 - 3 * n_heads, NB), f32)], axis=0)
    box_cols = boxes.T
    context, ctxt, lse = attend(queries, keys_all, values_all, tables, lengths, box_cols, boxes)
    mixed = inputs + lax.psum_scatter(
        dot(context, w_attn_out).astype(bf16), "mp", scatter_dimension=0, tiled=True
    ).astype(f32)
    normed_ffn = lax.all_gather(rms_norm(mixed, norm_ffn).astype(bf16), "mp", axis=0, tiled=True)
    gate_proj = dot(normed_ffn, w_gate)
    up_proj = dot(normed_ffn, w_up)
    hidden = gated_unit(gate_proj, up_proj).astype(bf16)
    result = mixed + lax.psum_scatter(
        dot(hidden, w_down).astype(bf16), "mp", scatter_dimension=0, tiled=True
    ).astype(f32)
    d_out = cotangent.astype(f32)
    d_full = lax.all_gather(cotangent, "mp", axis=0, tiled=True)
    d_hidden = contract(d_full, w_down, 1, 1)
    grad_down_t = contract(d_full, hidden, 0, 0)
    _, gelu_pull = jax.vjp(gated_unit, gate_proj, up_proj)
    d_gate, d_up = gelu_pull(d_hidden)
    d_gate = d_gate.astype(bf16)
    d_up = d_up.astype(bf16)
    grad_gate = contract(normed_ffn, d_gate, 0, 0)
    grad_up = contract(normed_ffn, d_up, 0, 0)
    ffn_grads = jnp.stack([g.astype(bf16).reshape(lax.axis_size("dp"), -1, g.shape[1]) for g in (grad_gate, grad_up, grad_down_t)], axis=1)
    ffn_sums = lax.psum_scatter(ffn_grads, "dp", scatter_dimension=0, tiled=True)[0].astype(f32)
    d_normed_ffn = lax.psum_scatter(
        (contract(d_gate, w_gate, 1, 1) + contract(d_up, w_up, 1, 1)).astype(bf16),
        "mp", scatter_dimension=0, tiled=True,
    ).astype(f32)
    _, norm_pull = jax.vjp(rms_norm, mixed, norm_ffn)
    d_mixed_part, grad_norm_ffn = norm_pull(d_normed_ffn)
    d_mixed = d_out + d_mixed_part
    d_attn = lax.all_gather(d_mixed.astype(bf16), "mp", axis=0, tiled=True)
    d_context = contract(d_attn, w_attn_out, 1, 1).astype(bf16)
    grad_out_t = contract(d_attn, context, 0, 0)
    d_queries, d_keys, d_values, d_tab = attend_back(
        queries, keys_all, values_all, d_context, ctxt, lse, tables, lengths, box_cols, boxes
    )
    grad_query = contract(normed, d_queries, 0, 0)
    grad_key = contract(normed, d_keys, 0, 0)
    grad_value = contract(normed, d_values, 0, 0)
    attn_grads = jnp.stack([g.astype(bf16).reshape(lax.axis_size("dp"), -1, g.shape[1]) for g in (grad_query, grad_key, grad_value, grad_out_t)], axis=1)
    attn_sums = lax.psum_scatter(attn_grads, "dp", scatter_dimension=0, tiled=True)[0].astype(f32)
    total_rows = contract(d_queries, w_query, 1, 1)
    total_rows = total_rows + contract(d_keys, w_key, 1, 1)
    d_normed = lax.psum_scatter(
        (total_rows + contract(d_values, w_value, 1, 1)).astype(bf16),
        "mp", scatter_dimension=0, tiled=True,
    ).astype(f32)
    _, first_pull = jax.vjp(rms_norm, inputs, norm_attn)
    d_inputs_part, grad_norm_attn = first_pull(d_normed)
    d_tokens = d_mixed + d_inputs_part
    n_dp = lax.axis_size("dp")
    gains = jnp.stack([grad_norm_attn.reshape(n_dp * lax.axis_size("mp"), -1), grad_norm_ffn.reshape(n_dp * lax.axis_size("mp"), -1)], axis=1)
    gains = lax.all_to_all(gains, ("dp", "mp"), split_axis=0, concat_axis=0, tiled=True).sum(axis=0)
    tabs = d_tab[:, : 3 * n_heads].reshape(n_dp, -1, 3, n_heads)
    tabs = lax.all_to_all(tabs, "dp", split_axis=0, concat_axis=0, tiled=True).sum(axis=0)
    return (
        result, d_tokens,
        attn_sums[0], attn_sums[1], attn_sums[2], attn_sums[3].T,
        ffn_sums[0], ffn_sums[1], ffn_sums[2].T,
        gains[0], gains[1], tabs[:, 0], tabs[:, 1], tabs[:, 2],
    )


def solution(mesh):
    in_specs = (
        P(("dp", "mp"), None),
        P(None, "mp"),
        P(None, "mp"),
        P(None, "mp"),
        P("mp", None),
        P(None, "mp"),
        P(None, "mp"),
        P("mp", None),
        P(),
        P(),
        P(None, "mp"),
        P(None, "mp"),
        P(None, "mp"),
        P("dp", None),
        P(None, "dp"),
        P(("dp", "mp"), None),
    )
    out_specs = (
        P(("dp", "mp"), None),
        P(("dp", "mp"), None),
        P("dp", "mp"),
        P("dp", "mp"),
        P("dp", "mp"),
        P("mp", "dp"),
        P("dp", "mp"),
        P("dp", "mp"),
        P("mp", "dp"),
        P(("dp", "mp")),
        P(("dp", "mp")),
        P("dp", "mp"),
        P("dp", "mp"),
        P("dp", "mp"),
    )
    return jax.shard_map(local, mesh=mesh, in_specs=in_specs, out_specs=out_specs, check_vma=False)
```

time: 5020 us -> 473 us (0.09); the launches traced: 4930 us -> 465 us
  local copies, waits for them, and re-layouts: 4290 us -> 16.8 us
  matrix products: 180 us -> 55 us
  other arithmetic: 117 us -> 27.1 us
  blocking collectives: 73.4 us -> 0 us
  Pallas kernels: 0 us -> 60.4 us
    gather x4 -> x0, local copies, waits for them, and re-layouts: 4060 us -> none  [the longest x2 4050 us: relative_bias(): return jnp.transpose(jnp.take(rel_table, bucket_grid, axis=0), (2, 0, 1))]
    unnamed x135 -> x81, local copies, waits for them, and re-layouts: 176 us -> 9.46 us
    unnamed x19 -> x10, waiting for transfers between devices: 139 us -> 0.67 us
    dot_general x26 -> x7, matrix products: 143 us -> 22.8 us  [dot(): return jnp.dot(a, b, preferred_element_type=f32)]
    reduce_scatter x5 -> x4, waiting for transfers between devices: 34.2 us -> 139 us  [the longest x1 62.1 us: local(): lax.psum_scatter(attn_grads, 'dp', scatter_dimension=0, tiled=True)[0]]
    unnamed x2 -> x0, blocking collectives: 73.4 us -> none
    pallas_call x0 -> x2, Pallas kernels: none -> 60.4 us  [the longest x1 43.2 us: attend_back(): pl.pallas_call(functools.partial(bwd_kernel, n_heads, qb), out_shape=(jax...]
    reshape x1 -> x2, local copies, waits for them, and re-layouts: 51.9 us -> 0.95 us  [local(): tabs = d_tab[:, :3 * n_heads].reshape(n_dp, -1, 3, n_heads)]
  transfers between devices with their start and end apart: 15 -> 12, of which waited for: 8 -> 11; matrix products, arithmetic and copies ran while one was open for 91% -> 12% of each run, Pallas kernels for 0% -> 9%
where the time goes in v1:
time: 473 us; the launch traced here: 465 us
  waiting for transfers between devices  278 us (59%)
  Pallas kernels  60.4 us (13%)
  matrix products  55 us (12%)
  other arithmetic  27.1 us (6%)
  local copies, waits for them, and re-layouts  16.8 us (4%)
  between operations  14.8 us (3%)
  starting transfers between devices  12.8 us (3%)
    reduce_scatter x1, waiting for transfers between devices, local(): lax.psum_scatter(attn_grads, 'dp', scatter_dimension=0, tiled=True)[0]  62.1 us
    pallas_call x1, Pallas kernels, attend_back(): pl.pallas_call(functools.partial(bwd_kernel, n_heads, qb), out_shape=(jax...  43.2 us
    reduce_scatter x1, waiting for transfers between devices, local(): lax.psum_scatter(dot(context, w_attn_out).astype(bf16), 'mp', scatter_dim...  33.3 us
    dot_general x14, matrix products, contract(): lax.dot_general(left_arr, right_arr, (((left_dim,), (right_dim,)), ((), (...  32.2 us
    reduce_scatter x1, waiting for transfers between devices, local(): lax.psum_scatter((contract(d_gate, w_gate, 1, 1) + contract(d_up, w_up, 1...  31.5 us
    reduce_scatter x1, waiting for transfers between devices, local(): lax.psum_scatter((total_rows + contract(d_values, w_value, 1, 1)).astype(...  31.1 us
    reduce_scatter x1, waiting for transfers between devices, local(): lax.psum_scatter(dot(hidden, w_down).astype(bf16), 'mp', scatter_dimensio...  30.3 us
    all_gather x1, waiting for transfers between devices, local(): lax.all_gather(rms_norm(inputs, norm_attn).astype(bf16), 'mp', axis=0, ti...  23.6 us
  transfers between devices with their start and end apart: 12, of which 11 were waited for; matrix products, arithmetic and copies ran while one was open for 12% of the time, Pallas kernels for 9%

profile of v1, /device:TPU:0, one launch (start us, length us, event | category | flops | bytes accessed | tf_op | source)
XLA Modules:
  0.0 465.4 jit_solution(17093602161825578384)
XLA Ops:
  7.3 1.3 fusion.20
  9.8 2.0 fusion.14
  11.9 1.0 copy.78
  13.0 0.7 maximum_maximum_fusion.tab_ref
  13.7 23.6 %all-gather.5.cloned.1.call-done = bf16[1024,1024]{1,0:T(8,128)(2,1)} async-done(((bf16[256,1024]{1,0:T(8,128)(2,1)}), bf16[1024,1024]{1,0:T(8,128)(2,1)}) %all-gather.5.cloned.1.call-update) | async-done | bytes 2097168 | tf_op jit(solution)/shard_map/all_gather | solution.py:384
  37.3 3.3 convolution_convert_fusion.10.v_ref
  40.5 1.5 convolution_convert_fusion.11.k_ref
  42.0 1.5 convolution_convert_fusion.12.q_ref
  43.6 17.2 %attend.1 = (bf16[1024,256]{1,0:T(8,128)(2,1)}, f32[256,1024]{1,0:T(8,128)}, f32[8,1024]{1,0:T(8,128)}) custom-call(s32[1,2]{1,0:T(1,128)} %lens.3, f32[16,32]{1,0:T(8,128)} %maximum_maximum_fusion.tab_ref, s32[1024,2]{1,0:T(8,128)} %bitcast.106, s32[2,1024]{1,0:T(2,128)} %box_rows.3, bf16[1024,256]{1,0:T(8,128)(2,1)} %convolution_convert_fusion.12.q_ref, ...), custom_call_target="tpu_custom_call" | custom-call | flops 17179869184 | bytes 4194304 | tf_op jit(solution)/shard_map/attend/pallas_call | solution.py:183
  60.8 3.2 convolution_convert_fusion
  64.1 33.3 %reduce-scatter.7.cloned.1.call-done = bf16[256,1024]{1,0:T(8,128)(2,1)} async-done(((bf16[1024,1024]{1,0:T(8,128)(2,1)}), bf16[256,1024]{1,0:T(8,128)(2,1)}) %reduce-scatter.7.cloned.1.call-update) | async-done | bytes 524304 | tf_op jit(solution)/shard_map/reduce_scatter | solution.py:392
  97.3 1.3 multiply_reduce_fusion
  98.7 2.0 multiply_convert_fusion.2
  101.8 21.6 %all-gather.7.cloned.1.call-done = bf16[1024,1024]{1,0:T(8,128)(2,1)} async-done(((bf16[256,1024]{1,0:T(8,128)(2,1)}), bf16[1024,1024]{1,0:T(8,128)(2,1)}) %all-gather.7.cloned.1.call-update) | async-done | bytes 2097168 | tf_op jit(solution)/shard_map/all_gather | solution.py:395
  123.5 5.4 %fusion.27 = f32[1024,704]{0,1:T(8,128)} fusion(bf16[1024,1024]{1,0:T(8,128)(2,1)} %all-gather.7.cloned.1.call-done, bf16[1024,704]{0,1:T(8,128)(2,1)} %param.22), kind=kOutput, calls=%fused_computation.78 | convolution fusion | flops 1476395008 | bytes 6422528 | tf_op jit(solution)/shard_map/dot_general | solution.py:21
  128.8 3.4 fusion.26
  132.2 15.4 %all-gather.9.cloned.1.call-done = bf16[1024,1024]{1,0:T(8,128)(2,1)} async-done(((bf16[256,1024]{1,0:T(8,128)(2,1)}), bf16[1024,1024]{1,0:T(8,128)(2,1)}) %all-gather.9.cloned.1.call-update) | async-done | bytes 2097168 | tf_op jit(solution)/shard_map/all_gather | solution.py:403
  147.6 7.3 %multiply_convert_fusion = (bf16[1024,704]{0,1:T(8,128)(2,1)S(1)}, bf16[1024,704]{0,1:T(8,128)(2,1)S(1)}, bf16[1024,704]{0,1:T(8,128)(2,1)}) fusion(f32[1024,704]{0,1:T(8,128)} %fusion.26, f32[1024,704]{0,1:T(8,128)} %fusion.27, bf16[1024,1024]{1,0:T(8,128)(2,1)} %all-gather.9.cloned.1.call-done, bf16[704,1024]{1,0:T(8,128)(2,1)S(1)} %copy-done), kind=kOutput, calls=%fused_computation.12 | convolution fusion | flops 1495138304 | bytes 13631488 | tf_op jit(solution)/shard_map/dot_general | solution.py:370
  154.9 1.8 fusion.28
  157.3 3.3 add_convert_fusion.1
  160.6 31.5 %reduce-scatter.11.cloned.1.call-done = bf16[256,1024]{1,0:T(8,128)(2,1)} async-done(((bf16[1024,1024]{1,0:T(8,128)(2,1)}), bf16[256,1024]{1,0:T(8,128)(2,1)}) %reduce-scatter.11.cloned.1.call-update) | async-done | bytes 524304 | tf_op jit(solution)/shard_map/reduce_scatter | solution.py:414
  192.2 2.1 fusion.16
  194.9 2.2 fusion.24
  197.2 3.7 fusion.7
  201.5 0.7 copy-done.35
  202.2 0.8 copy-done.30
  203.0 1.7 fusion.8
  205.3 1.2 copy-done.37
  206.5 1.7 fusion.9
  208.8 2.4 pad_maximum_fusion
  211.2 8.6 %all-gather.11.cloned.1.call-done = bf16[1024,1024]{1,0:T(8,128)(2,1)} async-done(((bf16[256,1024]{1,0:T(8,128)(2,1)}), bf16[1024,1024]{1,0:T(8,128)(2,1)}) %all-gather.11.cloned.1.call-update) | async-done | bytes 2097168 | tf_op jit(solution)/shard_map/all_gather | solution.py:421
  219.9 3.2 convolution_convert_fusion.9.do_ref
  223.1 43.2 %attend_back.1 = (bf16[1024,256]{1,0:T(8,128)(2,1)}, bf16[1024,256]{1,0:T(8,128)(2,1)}, bf16[1024,256]{1,0:T(8,128)(2,1)}, f32[32,16]{1,0:T(8,128)}) custom-call(s32[1,2]{1,0:T(1,128)} %lens.3, f32[16,32]{1,0:T(8,128)} %maximum_maximum_fusion.tab_ref, s32[1024,2]{1,0:T(8,128)} %bitcast.107, s32[2,1024]{1,0:T(2,128)} %box_rows.3, ...), custom_call_target="tpu_custom_call" | custom-call | flops 34359738368 | bytes 8388608 | tf_op jit(solution)/shard_map/attend_back/pallas_call | solution.py:323
  266.3 1.9 fusion.30
  268.2 0.7 fusion.29
  269.5 2.0 add_convert_fusion
  271.6 2.6 convolution_convert_fusion.5
  274.2 0.8 convolution_convert_fusion.8
  275.3 0.8 convolution_convert_fusion.7
  276.0 0.8 convolution_convert_fusion.6
  276.8 1.7 pad_maximum_fusion.1
  278.6 4.6 convolution_convert_fusion.1
  283.2 0.7 copy-done.19
  283.9 0.9 copy.88
  284.8 7.2 %all-to-all-start.1 = ((f32[8,4,3,4]{1,3,2,0:T(4,128)}), f32[8,4,3,4]{1,3,2,0:T(4,128)S(1)}, u32[]{:S(2)}, u32[]{:S(2)}) async-start(f32[8,4,3,4]{1,3,2,0:T(4,128)} %copy.88), calls=%async_computation.7 | async-start | bytes 98304 | tf_op jit(solution)/shard_map/all_to_all | solution.py:445
  292.1 7.1 %all-to-all-done.1 = f32[8,4,3,4]{1,3,2,0:T(4,128)S(1)} async-done(((f32[8,4,3,4]{1,3,2,0:T(4,128)}), f32[8,4,3,4]{1,3,2,0:T(4,128)S(1)}, u32[]{:S(2)}, u32[]{:S(2)}) %all-to-all-start.1) | async-done | bytes 1568 | tf_op jit(solution)/shard_map/all_to_all | solution.py:445
  299.3 0.7 copy.92
  300.0 0.7 copy.91
  301.3 13.1 %reduce-scatter.17.cloned.1.call-done = bf16[1,3,128,704]{2,3,1,0:T(8,128)(2,1)} async-done(((bf16[8,3,128,704]{2,3,1,0:T(8,128)(2,1)}), bf16[1,3,128,704]{2,3,1,0:T(8,128)(2,1)}) %reduce-scatter.17.cloned.1.call-update) | async-done | bytes 540688 | tf_op jit(solution)/shard_map/reduce_scatter | solution.py:413
  314.4 1.1 convert_element_type.121
  315.5 1.0 slice_bitcast_fusion
  316.5 31.1 %reduce-scatter.13.cloned.1.call-done = bf16[256,1024]{1,0:T(8,128)(2,1)} async-done(((bf16[1024,1024]{1,0:T(8,128)(2,1)}), bf16[256,1024]{1,0:T(8,128)(2,1)}) %reduce-scatter.13.cloned.1.call-update) | async-done | bytes 524304 | tf_op jit(solution)/shard_map/reduce_scatter | solution.py:434
  347.6 2.1 fusion.17
  349.7 1.4 stack_reshape.34
  351.1 1.4 pad_maximum_fusion.2
  352.5 4.7 %all-to-all-start = ((f32[32,2,32]{2,1,0:T(2,128)}), f32[32,2,32]{2,1,0:T(2,128)}, u32[]{:S(2)}, u32[]{:S(2)}) async-start(f32[32,2,32]{2,1,0:T(2,128)} %pad_maximum_fusion.2), calls=%async_computation.6 | async-start | bytes 65536 | tf_op jit(solution)/shard_map/all_to_all | solution.py:443
  357.2 62.1 %reduce-scatter.15.cloned.1.call-done = bf16[1,4,128,256]{3,2,1,0:T(8,128)(2,1)} async-done(((bf16[8,4,128,256]{3,2,1,0:T(8,128)(2,1)}), bf16[1,4,128,256]{3,2,1,0:T(8,128)(2,1)}) %reduce-scatter.15.cloned.1.call-update) | async-done | bytes 262160 | tf_op jit(solution)/shard_map/reduce_scatter | solution.py:431
  419.3 1.8 convert_element_type.116
  421.1 0.7 multiply_multiply_fusion.3
  421.8 30.3 %reduce-scatter.9.cloned.1.call-done = bf16[256,1024]{1,0:T(8,128)(2,1)} async-done(((bf16[1024,1024]{1,0:T(8,128)(2,1)}), bf16[256,1024]{1,0:T(8,128)(2,1)}) %reduce-scatter.9.cloned.1.call-update) | async-done | bytes 524304 | tf_op jit(solution)/shard_map/reduce_scatter | solution.py:399
  452.1 3.4 fusion.19
  455.5 0.8 slice_bitcast_fusion.3
  456.2 0.8 copy.93
  457.0 0.8 reduce_sum.79
  (110 shorter events, 7.9 us)
Async XLA Ops:
  7.2 140.4 %copy-start = (bf16[704,1024]{1,0:T(8,128)(2,1)S(1)}, bf16[704,1024]{1,0:T(8,128)(2,1)}, u32[]{:S(2)}) copy-start(bf16[704,1024]{1,0:T(8,128)(2,1)} %param.23) | copy-start | bytes 4325380
  7.2 4.7 %copy-start.23 = (s32[2,1024]{1,0:T(2,128)S(1)}, s32[2,1024]{1,0:T(2,128)}, u32[]{:S(2)}) copy-start(s32[2,1024]{1,0:T(2,128)} %box_rows.3) | copy-start | bytes 24580
  7.2 5.8 %copy-start.24 = (f32[32,4]{0,1:T(4,128)S(1)}, f32[32,4]{0,1:T(4,128)}, u32[]{:S(2)}) copy-start(f32[32,4]{0,1:T(4,128)} %param.28) | copy-start | bytes 1540
  7.2 5.8 %copy-start.25 = (f32[32,4]{0,1:T(4,128)S(1)}, f32[32,4]{0,1:T(4,128)}, u32[]{:S(2)}) copy-start(f32[32,4]{0,1:T(4,128)} %param.27) | copy-start | bytes 1540
  7.2 5.8 %copy-start.26 = (f32[32,4]{0,1:T(4,128)S(1)}, f32[32,4]{0,1:T(4,128)}, u32[]{:S(2)}) copy-start(f32[32,4]{0,1:T(4,128)} %param.26) | copy-start | bytes 1540
  7.2 30.0 %copy-start.9 = (bf16[1024,256]{1,0:T(8,128)(2,1)S(1)}, bf16[1024,256]{1,0:T(8,128)(2,1)}, u32[]{:S(2)}) copy-start(bf16[1024,256]{1,0:T(8,128)(2,1)} %param.19) | copy-start | bytes 1572868
  7.2 30.0 %all-gather.5.cloned.1.call-start = ((), (), s32[]{:S(2)}) async-start(), calls=%async_computation.8 | async-start | bytes 2621440 | tf_op jit(solution)/shard_map/all_gather | solution.py:384
  8.6 0.5 copy-start.22
  9.2 0.6 copy-start.20
  11.8 85.5 %reduce-scatter.7.cloned.1.call-start = ((), (), s32[]{:S(2)}) async-start(), calls=%async_computation.9 | async-start | bytes 2621440 | tf_op jit(solution)/shard_map/reduce_scatter | solution.py:392
  13.7 26.9 %copy-start.6 = (bf16[1024,256]{1,0:T(8,128)(2,1)S(1)}, bf16[1024,256]{1,0:T(8,128)(2,1)}, u32[]{:S(2)}) copy-start(bf16[1024,256]{1,0:T(8,128)(2,1)} %param.18) | copy-start | bytes 1572868
  37.3 3.3 copy-start.27
  40.5 1.5 copy-start.7
  43.6 17.2 %copy-start.15 = (bf16[256,1024]{1,0:T(8,128)(2,1)S(1)}, bf16[256,1024]{1,0:T(8,128)(2,1)}, u32[]{:S(2)}) copy-start(bf16[256,1024]{1,0:T(8,128)(2,1)} %param.20) | copy-start | bytes 1572868
  60.8 36.6 %copy-start.1 = (bf16[256,1024]{1,0:T(8,128)(2,1)S(1)}, bf16[256,1024]{1,0:T(8,128)(2,1)}, u32[]{:S(2)}) copy-start(bf16[256,1024]{1,0:T(8,128)(2,1)} %param.16) | copy-start | bytes 1572868
  64.0 34.6 %copy-start.16 = (f32[1024]{0:T(1024)S(1)}, f32[1024]{0:T(1024)}, u32[]{:S(2)}) copy-start(f32[1024]{0:T(1024)} %param.25) | copy-start | bytes 12292
  64.0 59.4 %all-gather.7.cloned.1.call-start = ((), (), s32[]{:S(2)}) async-start(), calls=%async_computation.10 | async-start | bytes 2621440 | tf_op jit(solution)/shard_map/all_gather | solution.py:395
  98.6 95.6 %copy-start.17 = (f32[256]{0:T(256)}, f32[256]{0:T(256)S(1)}, u32[]{:S(2)}) copy-start(f32[256]{0:T(256)S(1)} %fusion.23) | copy-start | bytes 3076
  100.7 46.8 %all-gather.9.cloned.1.call-start = ((), (), s32[]{:S(2)}) async-start(), calls=%async_computation.12 | async-start | bytes 2621440 | tf_op jit(solution)/shard_map/all_gather | solution.py:403
  101.3 90.9 %reduce-scatter.11.cloned.1.call-start = ((), (), s32[]{:S(2)}) async-start(), calls=%async_computation.13 | async-start | bytes 2621440 | tf_op jit(solution)/shard_map/reduce_scatter | solution.py:414
  123.5 5.4 %copy-start.29 = (bf16[1024,1024]{1,0:T(8,128)(2,1)S(1)}, bf16[1024,1024]{1,0:T(8,128)(2,1)}, u32[]{:S(2)}) copy-start(bf16[1024,1024]{1,0:T(8,128)(2,1)} %all-gather.7.cloned.1.call-done) | copy-start | bytes 6291460
  123.5 5.4 %copy-start.31 = (bf16[1024,704]{0,1:T(8,128)(2,1)S(1)}, bf16[1024,704]{0,1:T(8,128)(2,1)}, u32[]{:S(2)}) copy-start(bf16[1024,704]{0,1:T(8,128)(2,1)} %param.21) | copy-start | bytes 4325380
  147.6 7.3 %copy-start.32 = (bf16[1024,704]{0,1:T(8,128)(2,1)S(1)}, bf16[1024,704]{0,1:T(8,128)(2,1)}, u32[]{:S(2)}) copy-start(bf16[1024,704]{0,1:T(8,128)(2,1)} %param.21) | copy-start | bytes 4325380
  154.9 1.9 copy-start.34
  154.9 1.9 copy-start.36
  154.9 2.4 copy-start.33
  160.5 31.6 %copy-start.2 = (bf16[256,1024]{1,0:T(8,128)(2,1)S(1)}, bf16[256,1024]{1,0:T(8,128)(2,1)}, u32[]{:S(2)}) copy-start(bf16[256,1024]{1,0:T(8,128)(2,1)} %reduce-scatter.7.cloned.1.call-done) | copy-start | bytes 1572868
  160.5 34.3 %copy-start.3 = (bf16[256,1024]{1,0:T(8,128)(2,1)S(1)}, bf16[256,1024]{1,0:T(8,128)(2,1)}, u32[]{:S(2)}) copy-start(bf16[256,1024]{1,0:T(8,128)(2,1)} %param.31) | copy-start | bytes 1572868
  160.6 59.3 %all-gather.11.cloned.1.call-start = ((), (), s32[]{:S(2)}) async-start(), calls=%async_computation.14 | async-start | bytes 2621440 | tf_op jit(solution)/shard_map/all_gather | solution.py:421
  194.3 0.6 copy-start.21
  197.1 117.3 %reduce-scatter.17.cloned.1.call-start = ((), (), s32[]{:S(2)}) async-start(), calls=%async_computation.17 | async-start | bytes 4866048 | tf_op jit(solution)/shard_map/reduce_scatter | solution.py:413
  200.9 1.4 copy-start.35
  201.3 1.7 copy-start.30
  205.1 1.4 copy-start.37
  211.2 136.5 %reduce-scatter.13.cloned.1.call-start = ((), (), s32[]{:S(2)}) async-start(), calls=%async_computation.15 | async-start | bytes 2621440 | tf_op jit(solution)/shard_map/reduce_scatter | solution.py:434
  266.3 1.9 copy-start.8
  266.3 1.9 copy-start.13
  268.2 1.1 copy-start.10
  268.2 1.2 copy-start.11
  271.5 147.8 %reduce-scatter.15.cloned.1.call-start = ((), (), s32[]{:S(2)}) async-start(), calls=%async_computation.16 | async-start | bytes 2359296 | tf_op jit(solution)/shard_map/reduce_scatter | solution.py:431
  271.6 2.6 copy-start.14
  271.6 2.6 copy-start.28
  274.2 1.1 copy-start.12
  278.5 173.6 %reduce-scatter.9.cloned.1.call-start = ((), (), s32[]{:S(2)}) async-start(), calls=%async_computation.11 | async-start | bytes 2621440 | tf_op jit(solution)/shard_map/reduce_scatter | solution.py:399
  283.1 0.7 copy-start.19
  283.1 8.9 %copy-start.18 = (f32[1024]{0:T(1024)S(1)}, f32[1024]{0:T(1024)}, u32[]{:S(2)}) copy-start(f32[1024]{0:T(1024)} %get-tuple-element.84) | copy-start | bytes 12292
  284.8 14.5 %all-to-all-start.1 = ((f32[8,4,3,4]{1,3,2,0:T(4,128)}), f32[8,4,3,4]{1,3,2,0:T(4,128)S(1)}, u32[]{:S(2)}, u32[]{:S(2)}) async-start(f32[8,4,3,4]{1,3,2,0:T(4,128)} %copy.88), calls=%async_computation.7 | async-start | bytes 98304 | tf_op jit(solution)/shard_map/all_to_all | solution.py:445
  315.5 136.6 %copy-start.4 = (bf16[256,1024]{1,0:T(8,128)(2,1)S(1)}, bf16[256,1024]{1,0:T(8,128)(2,1)}, u32[]{:S(2)}) copy-start(bf16[256,1024]{1,0:T(8,128)(2,1)} %reduce-scatter.11.cloned.1.call-done) | copy-start | bytes 1572868
  352.5 104.5 %all-to-all-start = ((f32[32,2,32]{2,1,0:T(2,128)}), f32[32,2,32]{2,1,0:T(2,128)}, u32[]{:S(2)}, u32[]{:S(2)}) async-start(f32[32,2,32]{2,1,0:T(2,128)} %pad_maximum_fusion.2), calls=%async_computation.6 | async-start | bytes 65536 | tf_op jit(solution)/shard_map/all_to_all | solution.py:443
  452.1 3.4 copy-start.5
Sparse Core Ops, SparseCore 0:
  11.9 25.2 all-gather.4
  64.1 33.1 reduce-scatter.6
  100.8 22.5 all-gather.6
  124.9 22.5 all-gather.8
  160.7 31.4 reduce-scatter.10
  197.2 22.5 all-gather.10
  223.4 90.8 reduce-scatter.16
  317.1 30.5 reduce-scatter.12
  351.2 68.0 reduce-scatter.14
  421.7 30.4 reduce-scatter.8
